TPU v7x, 1024 devices: a whole 4x4x32 slice. The times are simulated.
1024 devices in a mesh: ctx: 32 (over z_lo, core), head: 4 (over x), seq: 8 (over y, z_hi).
Axes of the slice: x: 4, y: 4, z: 32 (z_hi: 2, z_lo: 16; z = z_hi * 16 + z_lo), core: 2. Of those that a mesh axis runs over, the one named last changes fastest.
Arguments:
- queries: bfloat16 [32768, 64, 128], P(('seq', 'ctx'), 'head'), parts along dimension 0, may hold values from -100 to 100
- keys: bfloat16 [32768, 4, 128], P(('seq', 'ctx'), 'head'), parts along dimension 0, may hold values from -8 to 8
- values: bfloat16 [32768, 4, 128], P(('seq', 'ctx'), 'head'), parts along dimension 0, may hold values from -6 to 6
Outputs:
- attended: bfloat16 [32768, 64, 128], P(('seq', 'ctx'), 'head'), parts along dimension 0
There are 8 independent parts, one for each index of `seq`. A program takes and returns all parts, laid end to end along the dimension named above; each array names one. Nothing has to cross between parts.
All inputs are finite; a program needn't handle non-finite values.
Results may differ from a plain program's by a relative error of at most 0.0035.
Values may be sent and summed in bfloat16 or wider, within the bound.
A program may use at most 32 MiB of HBM per device.

v0:
```python
import math

import jax
import jax.numpy as jnp
from jax import lax
from jax.sharding import PartitionSpec as P


def local(queries, keys, values):
    row_count = queries.shape[0]
    dev_index = lax.axis_index("ctx")
    kv_heads = keys.shape[1]
    group_size = queries.shape[1] // kv_heads
    head_width = queries.shape[2]
    scale = 1.0 / math.sqrt(head_width)
    local_rows = jnp.arange(row_count, dtype=jnp.int32)
    query_places = dev_index * row_count + local_rows
    tile_rows = math.gcd(row_count, 16)
    tile_count = row_count // tile_rows
    grouped = queries.reshape(tile_count, tile_rows, kv_heads, group_size, head_width)
    tile_places = query_places.reshape(tile_count, tile_rows)
    tile_last = jnp.max(tile_places, axis=1)

    def absorb(state_now, query_tile, places_tile, key_block, value_block, key_places):
        top_old, total_old, numerator = state_now
        scores = (
            jnp.einsum("rkgd,nkd->rkgn", query_tile, key_block, preferred_element_type=jnp.float32)
            * scale
        )
        visible = key_places[None, None, None, :] <= places_tile[:, None, None, None]
        scores = jnp.where(visible, scores, -1e30)
        top_new = jnp.maximum(top_old, jnp.max(scores, axis=-1))
        weights = jnp.where(visible, jnp.exp(scores - top_new[..., None]), 0.0)
        rescale = jnp.exp(top_old - top_new)
        total_new = total_old * rescale + jnp.sum(weights, axis=-1)
        numerator = numerator * rescale[..., None] + jnp.einsum(
            "rkgn,nkd->rkgd",
            weights.astype(jnp.bfloat16),
            value_block,
            preferred_element_type=jnp.float32,
        )
        return (top_new, total_new, numerator)

    initial = (
        jnp.full((tile_count, tile_rows, kv_heads, group_size), -1e30, jnp.float32),
        jnp.zeros((tile_count, tile_rows, kv_heads, group_size), jnp.float32),
        jnp.zeros((tile_count, tile_rows, kv_heads, group_size, head_width), jnp.float32),
    )
    key_piece = lax.all_gather(keys, "ctx", axis=0, tiled=True)
    value_piece = lax.all_gather(values, "ctx", axis=0, tiled=True)
    piece_rows = key_piece.shape[0]
    block_keys = math.gcd(piece_rows, 512)
    block_count = piece_rows // block_keys

    def one_pair(turn, state_in):
        tile = turn // block_count
        offset = turn % block_count * block_keys
        key_block = lax.dynamic_slice_in_dim(key_piece, offset, block_keys, 0)
        value_block = lax.dynamic_slice_in_dim(value_piece, offset, block_keys, 0)
        key_places = offset + jnp.arange(block_keys, dtype=jnp.int32)
        query_tile = lax.dynamic_index_in_dim(grouped, tile, 0, keepdims=False)
        places_tile = lax.dynamic_index_in_dim(tile_places, tile, 0, keepdims=False)
        tile_state = tuple(
            (
                lax.dynamic_index_in_dim(part_state, tile, 0, keepdims=False)
                for part_state in state_in
            )
        )

        def compute(state_keep):
            fresh = absorb(state_keep, query_tile, places_tile, key_block, value_block, key_places)
            return tuple(
                (
                    lax.dynamic_update_index_in_dim(whole_state, new_part, tile, 0)
                    for whole_state, new_part in zip(state_in, fresh)
                )
            )

        return lax.cond(
            jnp.min(key_places) > tile_last[tile], lambda state_keep: state_in, compute, tile_state
        )

    top_final, total_final, numerator = lax.fori_loop(
        0, tile_count * block_count, one_pair, initial
    )
    attended = (
        (numerator / total_final[..., None])
        .reshape(row_count, kv_heads * group_size, head_width)
        .astype(jnp.bfloat16)
    )
    return attended


def solution(mesh):
    return jax.shard_map(
        local,
        mesh=mesh,
        in_specs=(
            P(("seq", "ctx"), "head", None),
            P(("seq", "ctx"), "head", None),
            P(("seq", "ctx"), "head", None),
        ),
        out_specs=P(("seq", "ctx"), "head", None),
        check_vma=False,
    )
```

profile of v0, /device:TPU:483, one launch (start us, length us, event | category | flops | bytes accessed | tf_op | source)
XLA Modules:
  0.0 1033.3 jit_solution(8847780632200154251)
XLA Ops:
  8.1 328.4 %all-gather.3.cloned.1.call-done = bf16[4096,1,128]{2,0,1:T(8,128)(2,1)} async-done(((bf16[128,1,128]{2,0,1:T(8,128)(2,1)}), bf16[4096,1,128]{2,0,1:T(8,128)(2,1)}) %all-gather.3.cloned.1.call-update) | async-done | bytes 1048592 | tf_op jit(solution)/shard_map/all_gather | solution.py:49
  336.5 328.2 %all-gather.5.cloned.1.call-done = bf16[4096,1,128]{2,0,1:T(8,128)(2,1)} async-done(((bf16[128,1,128]{2,0,1:T(8,128)(2,1)}), bf16[4096,1,128]{2,0,1:T(8,128)(2,1)}) %all-gather.5.cloned.1.call-update) | async-done | bytes 1048592 | tf_op jit(solution)/shard_map/all_gather | solution.py:50
  664.8 360.6 %while.20 = (s32[]{:T(128)}, f32[8,16,1,16]{3,1,2,0:T(8,128)S(1)}, f32[8,16,1,16]{3,1,2,0:T(8,128)S(1)}, f32[8,16,1,16,128]{4,3,1,2,0:T(8,128)S(1)}, s32[8]{0:T(...) while((s32[]{:T(128)}, f32[8,16,1,16]{3,1,2,0:T(8,128)S(1)}, ...), condition=%wide.region_7.8_spmd.clone, body=%wide.region_1.7_spmd.clone.sunk | while | flops 68364952 | bytes 2550572 | solution.py:83
  667.5 2.9 conditional.3
  673.2 2.9 conditional.3
  678.8 2.9 conditional.3
  684.4 2.9 conditional.3
  690.1 2.9 conditional.3
  695.7 2.9 conditional.3
  701.3 2.9 conditional.3
  707.0 2.9 conditional.3
  712.6 2.9 conditional.3
  718.2 2.9 conditional.3
  723.9 2.9 conditional.3
  729.5 2.9 conditional.3
  735.1 2.9 conditional.3
  740.8 2.9 conditional.3
  746.4 2.9 conditional.3
  752.0 2.9 conditional.3
  757.7 2.9 conditional.3
  763.3 2.9 conditional.3
  768.9 2.9 conditional.3
  774.6 2.9 conditional.3
  780.2 2.9 conditional.3
  785.8 2.9 conditional.3
  791.5 2.9 conditional.3
  797.1 2.9 conditional.3
  802.7 2.9 conditional.3
  808.4 2.9 conditional.3
  814.0 2.9 conditional.3
  819.6 2.9 conditional.3
  825.3 2.9 conditional.3
  830.9 2.9 conditional.3
  836.5 2.9 conditional.3
  842.2 2.9 conditional.3
  847.8 2.9 conditional.3
  853.4 2.9 conditional.3
  859.1 2.9 conditional.3
  864.7 2.9 conditional.3
  870.3 2.9 conditional.3
  876.0 2.9 conditional.3
  881.6 2.9 conditional.3
  887.2 2.9 conditional.3
  892.9 2.9 conditional.3
  898.5 2.9 conditional.3
  904.1 2.9 conditional.3
  909.8 2.9 conditional.3
  915.4 2.9 conditional.3
  921.0 2.9 conditional.3
  926.7 2.9 conditional.3
  932.3 2.9 conditional.3
  937.9 2.9 conditional.3
  943.6 2.9 conditional.3
  949.2 2.9 conditional.3
  954.8 2.9 conditional.3
  960.5 2.9 conditional.3
  966.1 2.9 conditional.3
  971.7 2.9 conditional.3
  977.4 2.9 conditional.3
  983.0 2.9 conditional.3
  988.6 2.9 conditional.3
  994.3 2.9 conditional.3
  1011.2 2.9 conditional.3
  1016.8 2.9 conditional.3
  (908 shorter events, 278.2 us)
Async XLA Ops:
  6.5 330.0 %all-gather.3.cloned.1.call-start = ((), (), s32[]{:S(2)}) async-start(), calls=%async_computation | async-start | bytes 1081344 | tf_op jit(solution)/shard_map/all_gather | solution.py:49
  7.3 657.4 %all-gather.5.cloned.1.call-start = ((), (), s32[]{:S(2)}) async-start(), calls=%async_computation.1 | async-start | bytes 1081344 | tf_op jit(solution)/shard_map/all_gather | solution.py:50
Sparse Core Ops, SparseCore 0:
  10.0 326.4 all-gather.2
  339.2 325.4 all-gather.4
where the time goes:
time: 1040 us; the launch traced here: 1030 us
  waiting for transfers between devices  658 us (63%)
  matrix products  155 us (15%)
  loops' own time  93.9 us (9%)
  other arithmetic  68.6 us (7%)
  local copies, waits for them, and re-layouts  44.8 us (4%)
  between operations  13.4 us (1%)
    all_gather x1, waiting for transfers between devices, local(): key_piece = lax.all_gather(keys, 'ctx', axis=0, tiled=True)  328 us
    all_gather x1, waiting for transfers between devices, local(): value_piece = lax.all_gather(values, 'ctx', axis=0, tiled=True)  328 us
    another operation x1, loops' own time, local(): lax.fori_loop(0, tile_count * block_count, one_pair, initial)  88.1 us
    dot_general x64, matrix products, absorb(): jnp.einsum('rkgd,nkd->rkgn', query_tile, key_block, preferred_element_typ...  78.1 us
    dot_general x64, matrix products, absorb(): jnp.einsum('rkgn,nkd->rkgd', weights.astype(jnp.bfloat16), value_block, p...  76.5 us
    add x64, other arithmetic, one_pair(): key_places = offset + jnp.arange(block_keys, dtype=jnp.int32)  44.6 us
    dynamic_slice x64, local copies, waits for them, and re-layouts, one_pair(): tile_last[tile]  41.8 us
  transfers between devices with their start and end apart: 2, of which 2 were waited for; matrix products, arithmetic and copies ran while one was open for 0% of the time, Pallas kernels for 0%

commit v1 on v0

v1 whole, which is shorter than its diff:
```python
import functools
import math

import jax
import jax.numpy as jnp
from jax import lax
from jax.experimental import pallas as pl
from jax.experimental.pallas import tpu as pltpu
from jax.sharding import PartitionSpec as P

MESH = pl.DeviceIdType.MESH
TILE = 256
PIECES = 2
HALVES = 1
TABLE = (
    (416,),
    (545, 0),
    (674, 160, 1),
    (803, 9024, 289, 2),
    (932, 13249, 418, 3, 0),
    (1061, 17474, 547, 4, 544, 1),
    (1190, 21699, 676, 5, 21696, 673, 2),
    (1319, 25924, 805, 6, 25921, 802, 3, 0),
    (1448, 30149, 934, 7, 30146, 931, 4, 928, 1),
    (1577, 34374, 1063, 8, 34371, 1060, 34368, 5, 1057, 2),
    (1706, 38599, 1192, 9, 38596, 1189, 38593, 6, 1186, 3, 0),
    (1835, 42824, 1321, 10, 42821, 1318, 42818, 7, 1315, 4, 1312, 1),
    (1708, 46793, 1450, 11, 46790, 1447, 8, 46787, 1444, 46784, 5, 1441, 2),
    (1837, 1836, 51018, 1579, 1833, 51015, 1576, 1830, 51012, 1573, 1827, 51009, 1824, 1570),
    (1966, 1965, 55243, 1964, 1962, 55240, 1961, 1959, 55237, 1958, 1956, 55234, 1955, 1953, 1952),
    (15, 14, 13, 11, 12, 10, 8, 9, 7, 5, 6, 4, 2, 3, 1, 0),
)


def unpack(item):
    targets = [item // 128 // 32**i % 32 for i in range(item // 32 % 4)]
    return item % 16, item // 16 % 2, [(t % 16, t // 16) for t in targets]


def kernel(
    chips, group, q_hbm, k_hbm, v_hbm, o_ref,
    q_ref, k_ref, v_ref, m_ref, l_ref, acc_ref,
    load_sem, recv_sem, pair_sem, send_sem,
):
    me = lax.axis_index("ctx")
    seq = lax.axis_index("seq")
    chip, core = me // 2, me % 2
    rows = k_hbm.shape[0]
    piece_rows = rows // PIECES
    total_rows = q_ref.shape[0]
    factor = math.log2(math.e) / math.sqrt(q_ref.shape[1])

    def device(chip_at, core_at, other=0):
        return {"ctx": chip_at * 2 + core_at, "seq": seq + other * (1 - 2 * (seq % 2))}

    def rows_of(ref, slot, piece=None):
        start = slot * rows
        if piece is None:
            return ref.at[pl.ds(pl.multiple_of(start, rows), rows)]
        return ref.at[pl.ds(pl.multiple_of(start + piece * piece_rows, piece_rows), piece_rows)]

    loads = [
        pltpu.make_async_copy(k_hbm, rows_of(k_ref, me), load_sem.at[0]),
        pltpu.make_async_copy(v_hbm, rows_of(v_ref, me), load_sem.at[1]),
        pltpu.make_async_copy(q_hbm, q_ref, load_sem.at[2]),
    ]
    for load in loads:
        load.start()

    def pick(values):
        out = jnp.int32(values[0])
        for c in range(1, chips):
            if values[c] != values[0]:
                out = jnp.where(chip == c, values[c], out)
        return out

    senders = [set() for _ in range(chips)]
    receivers = [set() for _ in range(chips)]
    for c in range(chips):
        for item in TABLE[c]:
            for target, other in unpack(item)[2]:
                receivers[c].add((target, other))
                senders[target].add((c, other))
    barrier = pltpu.get_barrier_semaphore()
    for other in (1, 0):
        for c in range(chips):
            flags = [int((c, other) in senders[t]) for t in range(chips)]
            if any(flags):

                @pl.when(pick(flags) == 1)
                def _():
                    pl.semaphore_signal(barrier, inc=1, device_id=device(c, core, other), device_id_type=MESH)

    pl.semaphore_signal(barrier, inc=1, device_id=device(chip, 1 - core), device_id_type=MESH)
    longest = max(len(row) for row in TABLE)
    row = [pick([row[n] if n < len(row) else 0 for row in TABLE]) for n in range(longest)]

    def item_of(n):
        out = row[0]
        for i in range(1, longest):
            out = jnp.where(n == i, row[i], out)
        return out

    item_count = pick([len(row) for row in TABLE])
    for load in loads[:2]:
        load.wait()
    pl.semaphore_wait(barrier, 1 + pick([len(r) for r in receivers]))

    refs = (k_ref, v_ref)
    parts = [(kind, piece) for kind in range(2) for piece in range(PIECES)]
    degree = max(item // 32 % 4 for row in TABLE for item in row)

    def remote(here, there, n, arrived, target):
        return pltpu.make_async_remote_copy(
            src_ref=here, dst_ref=there, send_sem=send_sem.at[n], recv_sem=arrived,
            device_id=target, device_id_type=MESH,
        )

    def at_home(s):
        return 2 * s + core

    def away(s):
        return 2 * chips + s

    def send_on(n, item, kind, piece):
        s, foreign = item % 16, item // 16 % 2
        count = item // 32 % 4
        ref = refs[kind]
        here = rows_of(ref, jnp.where(foreign == 1, away(s), at_home(s)), piece)
        for i in range(degree):
            target = item // (128 * 32**i) % 32
            other = target // 16
            lands = jnp.logical_and(other == 1, foreign == 0)
            copy = remote(
                here,
                rows_of(ref, jnp.where(lands, away(s), at_home(s)), piece),
                n,
                recv_sem.at[jnp.where(lands, chips + s, s), kind, piece],
                device(target % 16, core, other),
            )
            pl.when(i < count)(copy.start)

    def across(n, s, kind):
        block = rows_of(refs[kind], at_home(s))
        return remote(block, block, n, pair_sem.at[s, kind], device(chip, 1 - core))

    def relay(n, item, kind):
        s, foreign = item % 16, item // 16 % 2
        for piece in range(PIECES):
            block = rows_of(refs[kind], jnp.where(foreign == 1, away(s), at_home(s)), piece)
            arrived = recv_sem.at[jnp.where(foreign == 1, chips + s, s), kind, piece]
            remote(block, block, n, arrived, device(chip, 1 - core)).wait_recv()
            send_on(n, item, kind, piece)
        pl.when(foreign == 0)(across(n, s, kind).start)

    def paired(s):
        for kind in range(2):
            block = rows_of(refs[kind], 2 * s + 1 - core)
            remote(block, block, 0, pair_sem.at[s, kind], device(chip, 1 - core)).wait_recv()

    def sent(n):
        item = item_of(n)
        count = item // 32 % 4 + 1 - item // 16 % 2
        for times in range(1, degree + 2):

            @pl.when(count == times)
            def _():
                bulk = k_ref.at[pl.ds(0, times * 2 * rows)]
                remote(bulk, bulk, n, pair_sem.at[0, 0], device(chip, 1 - core)).wait_send()

    for kind in range(2):
        for piece in range(PIECES):
            send_on(0, row[0], kind, piece)
        across(0, chip, kind).start()
    loads[2].wait()

    wide = 2 * rows
    tiles = total_rows // TILE

    def first(tile):
        at = pl.ds(tile * TILE, TILE)
        keys = pl.ds(pl.multiple_of(chip * wide, wide), wide)
        s = lax.dot_general(
            q_ref[at], k_ref[keys], (((1,), (1,)), ((), ())), preferred_element_type=jnp.float32
        )
        place = core * rows + (tile * TILE + lax.broadcasted_iota(jnp.int32, s.shape, 0)) // group
        s = jnp.where(lax.broadcasted_iota(jnp.int32, s.shape, 1) <= place, s, -1e30)
        top = jnp.max(s, axis=1, keepdims=True)
        p = jnp.exp2((s - top) * factor)
        m_ref[at] = jnp.broadcast_to(top, (TILE, 128))
        part = p[:, :128]
        for j in range(128, wide, 128):
            part += p[:, j : j + 128]
        l_ref[at] = part
        acc_ref[at] = jnp.dot(p.astype(jnp.bfloat16), v_ref[keys], preferred_element_type=jnp.float32)

    def absorb(tile, s_chip):
        at = pl.ds(tile * TILE, TILE)
        keys = pl.ds(pl.multiple_of(s_chip * wide, wide), wide)
        s = lax.dot_general(
            q_ref[at], k_ref[keys], (((1,), (1,)), ((), ())), preferred_element_type=jnp.float32
        )
        old = m_ref[at]
        top = jnp.maximum(old, jnp.max(s, axis=1, keepdims=True))
        shrink = jnp.exp2((old - top) * factor)
        m_ref[at] = top
        ps = []
        part = l_ref[at] * shrink
        for j in range(0, wide, 128):
            p = jnp.exp2((s[:, j : j + 128] - top) * factor)
            part += p
            ps.append(p.astype(jnp.bfloat16))
        l_ref[at] = part
        p = jnp.concatenate(ps, axis=1)
        acc_ref[at] = acc_ref[at] * shrink + jnp.dot(
            p, v_ref[keys], preferred_element_type=jnp.float32
        )

    paired(chip)
    for tile in range(tiles):
        first(tile)

    def half(i, s):
        for tile in range(i * tiles // HALVES, (i + 1) * tiles // HALVES):
            absorb(tile, s)

    def step(n, waiting):
        item = item_of(n)
        fresh = item // 16 % 2 == 0
        ready = jnp.logical_and(fresh, waiting >= 0)
        for kind in range(2):
            relay(n, item, kind)
            if HALVES == 2 or kind == 1:

                @pl.when(ready)
                def _():
                    if kind == HALVES % 2:
                        paired(waiting)
                    half(kind if HALVES == 2 else 0, waiting)

        return jnp.where(fresh, item % 16, waiting)

    waiting = lax.fori_loop(1, item_count, step, jnp.int32(-1))

    @pl.when(waiting >= 0)
    def _():
        paired(waiting)
        for i in range(HALVES):
            half(i, waiting)

    for tile in range(tiles):
        at = pl.ds(tile * TILE, TILE)
        total = jnp.sum(l_ref[at], axis=1, keepdims=True)
        o_ref[at] = (acc_ref[at] * (1.0 / total)).astype(o_ref.dtype)

    def finish(n, carry):
        sent(n)
        return carry

    lax.fori_loop(0, item_count, finish, 0)


def attend(ctx, queries, keys, values):
    count, heads, width = queries.shape
    group = heads // keys.shape[1]
    rows = count * group
    q = queries.reshape(rows, width)
    k = keys.reshape(count, width)
    v = values.reshape(count, width)
    chips = ctx // 2
    longest = max(len(row) for row in TABLE)
    far = [item % 16 for row in TABLE for item in row if item // 16 % 2]
    slots = ctx + max(far, default=-1) + 1
    anywhere = pl.BlockSpec(memory_space=pltpu.HBM)
    out = pl.pallas_call(
        functools.partial(kernel, chips, group),
        out_shape=jax.ShapeDtypeStruct((rows, width), queries.dtype),
        in_specs=[anywhere] * 3,
        out_specs=pl.BlockSpec(memory_space=pltpu.VMEM),
        scratch_shapes=[
            pltpu.VMEM((rows, width), queries.dtype),
            pltpu.VMEM((slots * count, width), keys.dtype),
            pltpu.VMEM((slots * count, width), values.dtype),
            pltpu.VMEM((rows, 128), jnp.float32),
            pltpu.VMEM((rows, 128), jnp.float32),
            pltpu.VMEM((rows, width), jnp.float32),
            pltpu.SemaphoreType.DMA((3,)),
            pltpu.SemaphoreType.DMA((slots - chips, 2, PIECES)),
            pltpu.SemaphoreType.DMA((chips, 2)),
            pltpu.SemaphoreType.DMA((longest,)),
        ],
        compiler_params=pltpu.CompilerParams(
            collective_id=0, has_side_effects=True, vmem_limit_bytes=32 * 1024 * 1024
        ),
        name="attend",
    )(*(pltpu.with_memory_space_constraint(a, pltpu.HBM) for a in (q, k, v)))
    return out.reshape(count, heads, width)


def solution(mesh):
    spec = P(("seq", "ctx"), "head", None)
    return jax.shard_map(
        functools.partial(attend, mesh.shape["ctx"]),
        mesh=mesh,
        in_specs=(spec, spec, spec),
        out_specs=spec,
        check_vma=False,
    )
```

time: 1040 us -> 43.3 us (0.04)
  the two profiles are of different devices: /device:TPU:483 before, /device:TPU:353 now
where the time goes in v1:
time: 43.3 us; the launch traced here: 43.1 us
  Pallas kernels  42.3 us (98%)
  local copies, waits for them, and re-layouts  0.8 us (2%)
    pallas_call x1, Pallas kernels, attend(): pl.pallas_call(functools.partial(kernel, chips, group), out_shape=jax.Sha...  42.3 us

profile of v1, /device:TPU:353, one launch (start us, length us, event | category | flops | bytes accessed | tf_op | source)
XLA Modules:
  0.0 43.1 jit_solution(18021317570535957800)
XLA Ops:
  0.0 42.3 %attend.1 = bf16[2048,128]{1,0:T(8,128)(2,1)S(1)} custom-call(bf16[2048,128]{1,0:T(8,128)(2,1)} %bitcast.5, bf16[128,128]{1,0:T(8,128)(2,1)} %bitcast.6, bf16[128,128]{1,0:T(8,128)(2,1)} %bitcast.7), custom_call_target="tpu_custom_call" | custom-call | tf_op jit(solution)/shard_map/attend/pallas_call | solution.py:275
  42.3 0.8 %copy.5 = bf16[128,16,128]{2,1,0:T(8,128)(2,1)} copy(bf16[128,16,128]{2,1,0:T(8,128)(2,1)S(1)} %bitcast.4) | data formatting | bytes 1048576

commit v2 on v1

--- a/solution.py
+++ b/solution.py
@@ -9,26 +9,27 @@
 from jax.sharding import PartitionSpec as P
 
 MESH = pl.DeviceIdType.MESH
-TILE = 256
-PIECES = 2
+TILE = 512
+PIECES = 1
+LATE = 5
 HALVES = 1
 TABLE = (
     (416,),
     (545, 0),
-    (674, 160, 1),
-    (803, 9024, 289, 2),
-    (932, 13249, 418, 3, 0),
-    (1061, 17474, 547, 4, 544, 1),
-    (1190, 21699, 676, 5, 21696, 673, 2),
-    (1319, 25924, 805, 6, 25921, 802, 3, 0),
-    (1448, 30149, 934, 7, 30146, 931, 4, 928, 1),
-    (1577, 34374, 1063, 8, 34371, 1060, 34368, 5, 1057, 2),
-    (1706, 38599, 1192, 9, 38596, 1189, 38593, 6, 1186, 3, 0),
-    (1835, 42824, 1321, 10, 42821, 1318, 42818, 7, 1315, 4, 1312, 1),
-    (1708, 46793, 1450, 11, 46790, 1447, 8, 46787, 1444, 46784, 5, 1441, 2),
-    (1837, 1836, 51018, 1579, 1833, 51015, 1576, 1830, 51012, 1573, 1827, 51009, 1824, 1570),
-    (1966, 1965, 55243, 1964, 1962, 55240, 1961, 1959, 55237, 1958, 1956, 55234, 1955, 1953, 1952),
-    (15, 14, 13, 11, 12, 10, 8, 9, 7, 5, 6, 4, 2, 3, 1, 0),
+    (674, 0, 1),
+    (803, 140128, 1, 2),
+    (932, 275425, 2, 3, 0),
+    (1061, 410722, 3, 4, 0, 1),
+    (1190, 546019, 4, 546016, 5, 1, 2),
+    (1319, 681316, 5, 681313, 6, 2, 3, 0),
+    (1448, 816613, 6, 816610, 7, 3, 4, 0, 1),
+    (1577, 951910, 7, 951907, 8, 4, 951904, 5, 1, 2),
+    (1706, 1087207, 8, 1087204, 9, 5, 1087201, 6, 2, 3, 0),
+    (1835, 1222504, 9, 1222501, 10, 6, 1222498, 7, 3, 4, 0, 1),
+    (1964, 1357801, 10, 1357798, 11, 1357795, 7, 8, 1357792, 4, 5, 1, 2),
+    (1837, 1492842, 11, 12, 1492839, 8, 9, 1492836, 5, 1492833, 6, 2, 3, 0),
+    (1966, 1965, 1628139, 12, 1962, 1628136, 9, 1959, 1628133, 6, 1956, 1628130, 3, 1953, 0),
+    (15, 14, 55116, 13, 11, 55113, 10, 8, 55110, 7, 5, 55107, 4, 55104, 2, 1),
 )
 
 
@@ -227,6 +228,7 @@
     def step(n, waiting):
         item = item_of(n)
         fresh = item // 16 % 2 == 0
+        pl.when(n >= LATE)(functools.partial(sent, n - LATE))
         ready = jnp.logical_and(fresh, waiting >= 0)
         for kind in range(2):
             relay(n, item, kind)
@@ -257,7 +259,7 @@
         sent(n)
         return carry
 
-    lax.fori_loop(0, item_count, finish, 0)
+    lax.fori_loop(jnp.maximum(item_count - LATE, 0), item_count, finish, 0)
 
 
 def attend(ctx, queries, keys, values):

time: 43.3 us -> 43.2 us (level)
  the two profiles are of different devices: /device:TPU:353 before, /device:TPU:443 now
where the time goes in v2:
time: 43.2 us; the launch traced here: 43.1 us
  Pallas kernels  42.3 us (98%)
  local copies, waits for them, and re-layouts  0.8 us (2%)
    pallas_call x1, Pallas kernels, attend(): pl.pallas_call(functools.partial(kernel, chips, group), out_shape=jax.Sha...  42.3 us

profile of v2, /device:TPU:443, one launch (start us, length us, event | category | flops | bytes accessed | tf_op | source)
XLA Modules:
  0.0 43.1 jit_solution(14656496456604233490)
XLA Ops:
  0.0 42.3 %attend.1 = bf16[2048,128]{1,0:T(8,128)(2,1)S(1)} custom-call(bf16[2048,128]{1,0:T(8,128)(2,1)} %bitcast.5, bf16[128,128]{1,0:T(8,128)(2,1)} %bitcast.6, bf16[128,128]{1,0:T(8,128)(2,1)} %bitcast.7), custom_call_target="tpu_custom_call" | custom-call | tf_op jit(solution)/shard_map/attend/pallas_call | solution.py:277
  42.3 0.8 %copy.5 = bf16[128,16,128]{2,1,0:T(8,128)(2,1)} copy(bf16[128,16,128]{2,1,0:T(8,128)(2,1)S(1)} %bitcast.4) | data formatting | bytes 1048576

commit v3 on v2

--- a/solution.py
+++ b/solution.py
@@ -17,19 +17,19 @@
     (416,),
     (545, 0),
     (674, 0, 1),
-    (803, 140128, 1, 2),
-    (932, 275425, 2, 3, 0),
-    (1061, 410722, 3, 4, 0, 1),
-    (1190, 546019, 4, 546016, 5, 1, 2),
-    (1319, 681316, 5, 681313, 6, 2, 3, 0),
-    (1448, 816613, 6, 816610, 7, 3, 4, 0, 1),
-    (1577, 951910, 7, 951907, 8, 4, 951904, 5, 1, 2),
-    (1706, 1087207, 8, 1087204, 9, 5, 1087201, 6, 2, 3, 0),
-    (1835, 1222504, 9, 1222501, 10, 6, 1222498, 7, 3, 4, 0, 1),
-    (1964, 1357801, 10, 1357798, 11, 1357795, 7, 8, 1357792, 4, 5, 1, 2),
-    (1837, 1492842, 11, 12, 1492839, 8, 9, 1492836, 5, 1492833, 6, 2, 3, 0),
-    (1966, 1965, 1628139, 12, 1962, 1628136, 9, 1959, 1628133, 6, 1956, 1628130, 3, 1953, 0),
-    (15, 14, 55116, 13, 11, 55113, 10, 8, 55110, 7, 5, 55107, 4, 55104, 2, 1),
+    (803, 267104, 1, 2),
+    (932, 402401, 2, 3, 0),
+    (1061, 537698, 3, 4, 0, 1),
+    (1190, 672995, 4, 672992, 5, 1, 2),
+    (1319, 808292, 5, 808289, 6, 2, 3, 0),
+    (1448, 943589, 6, 943586, 7, 3, 4, 0, 1),
+    (1577, 1078886, 7, 1078883, 8, 4, 1078880, 5, 1, 2),
+    (1706, 1214183, 8, 1214180, 9, 5, 1214177, 6, 2, 3, 0),
+    (1835, 1349480, 9, 1349477, 10, 6, 1349474, 7, 3, 4, 0, 1),
+    (1964, 1484777, 10, 1484774, 11, 1484771, 7, 8, 1484768, 4, 5, 1, 2),
+    (1837, 1619818, 11, 12, 1619815, 8, 9, 1619812, 5, 1619809, 6, 2, 3, 0),
+    (1966, 1965, 1755115, 12, 1962, 1755112, 9, 1959, 1755109, 6, 1956, 1755106, 3, 1953, 0),
+    (15, 14, 59084, 13, 11, 59081, 10, 8, 59078, 7, 5, 59075, 4, 59072, 2, 1),
 )
 
 

time: 43.2 us -> 43 us (level)
  no operation moved by 1% of the time
where the time goes in v3:
time: 43 us; the launch traced here: 42.9 us
  Pallas kernels  42.1 us (98%)
  local copies, waits for them, and re-layouts  0.8 us (2%)
    pallas_call x1, Pallas kernels, attend(): pl.pallas_call(functools.partial(kernel, chips, group), out_shape=jax.Sha...  42.1 us

profile of v3, /device:TPU:443, one launch (start us, length us, event | category | flops | bytes accessed | tf_op | source)
XLA Modules:
  0.0 42.9 jit_solution(7010301214450314663)
XLA Ops:
  0.0 42.1 %attend.1 = bf16[2048,128]{1,0:T(8,128)(2,1)S(1)} custom-call(bf16[2048,128]{1,0:T(8,128)(2,1)} %bitcast.5, bf16[128,128]{1,0:T(8,128)(2,1)} %bitcast.6, bf16[128,128]{1,0:T(8,128)(2,1)} %bitcast.7), custom_call_target="tpu_custom_call" | custom-call | tf_op jit(solution)/shard_map/attend/pallas_call | solution.py:277
  42.1 0.8 %copy.5 = bf16[128,16,128]{2,1,0:T(8,128)(2,1)} copy(bf16[128,16,128]{2,1,0:T(8,128)(2,1)S(1)} %bitcast.4) | data formatting | bytes 1048576
